TPU v7x, 128 devices: a whole 4x4x4 slice. The times are simulated.
128 devices in a mesh: pair: 8 (over x, core), ints: 16 (over y, z).
Axes of the slice: x: 4, y: 4, z: 4, core: 2. Of those that a mesh axis runs over, the one named last changes fastest.
Arguments:
- t2: bfloat16 [4096, 8192], P('pair', 'ints'), may hold values from -6 to 6
- t2_live: int32 [8, 64], P('pair', 'ints'), may hold values 0 or 1
- int_tiles: int32 [5120, 2], P('ints'), may hold values from 0 to 63
- integrals: bfloat16 [5120, 128, 128], P('ints'), may hold values from -0.0625 to 0.0625
- cycle_w: bfloat16 [4096, 4096], P('pair'), may hold values from -0.09375 to 0.09375
- res_live: int32 [8, 64], P('pair', 'ints'), may hold values 0 or 1
Outputs:
- residual: float32 [4096, 8192], P('pair', 'ints')
All inputs are finite; a program needn't handle non-finite values. No bound on the sum of `t2_live` or of `res_live` on one device may be relied on, other than what follows from the above.
Results may differ from a plain program's by a relative error of at most 0.0003.
Values may be sent and summed in bfloat16 or wider, within the bound.
No kernel may reach another device: no remote copies, remote signals or barrier semaphores. Data moves between devices by JAX's collectives and lax.ppermute only.
A program may use at most 192 MiB of HBM per device.

v0:
```python
import jax
import jax.numpy as jnp
from jax import lax
from jax.sharding import PartitionSpec as P


def local(t2, t2_live, int_tiles, integrals, cycle_w, res_live):
    rows_here = t2.shape[0]
    tile_size = integrals.shape[1]
    tiles_here = t2.shape[1] // tile_size
    live_mask = t2_live[0].astype(t2.dtype)
    amps = (t2.reshape(rows_here, tiles_here, tile_size) * live_mask[None, :, None]).reshape(
        rows_here, tiles_here * tile_size
    )
    block_amps = lax.all_gather(amps, "ints", axis=1, tiled=True)
    tiles_all = block_amps.shape[1] // tile_size
    amps_tiled = block_amps.reshape(rows_here, tiles_all, tile_size)
    count_here = integrals.shape[0]
    group_size = 64
    tile_groups = int_tiles.reshape(count_here // group_size, group_size, 2)
    int_groups = integrals.reshape(count_here // group_size, group_size, tile_size, tile_size)
    tile_ids = jnp.arange(tiles_all, dtype=jnp.int32)

    def ladder_step(partial_value, entry):
        pairs_uv, blocks = entry
        source_table = (pairs_uv[:, 0:1] == tile_ids[None, :]).astype(jnp.bfloat16)
        target_table = (pairs_uv[:, 1:2] == tile_ids[None, :]).astype(jnp.float32)
        picked = jnp.einsum(
            "jt,ptc->jpc", source_table, amps_tiled, preferred_element_type=jnp.float32
        ).astype(jnp.bfloat16)
        product = jnp.einsum("jpc,jcd->jpd", picked, blocks, preferred_element_type=jnp.float32)
        partial_value = partial_value + jnp.einsum(
            "jv,jpd->vpd", target_table, product, precision=lax.Precision.HIGHEST
        )
        return (partial_value, None)

    start_sum = jnp.zeros((tiles_all, rows_here, tile_size), jnp.float32)
    partial_value, _ = lax.scan(ladder_step, start_sum, (tile_groups, int_groups))
    summed = lax.psum(partial_value, "ints")
    owned = lax.dynamic_slice_in_dim(summed, lax.axis_index("ints") * tiles_here, tiles_here, 0)
    ladder = owned.transpose(1, 0, 2).reshape(rows_here, tiles_here * tile_size)
    cycle_term = jnp.dot(
        cycle_w,
        lax.all_gather(amps, "pair", axis=0, tiled=True),
        preferred_element_type=jnp.float32,
    )
    keep_mask = jnp.repeat(res_live[0], tile_size).astype(jnp.float32)[None, :]
    return keep_mask * (ladder + cycle_term)


def solution(mesh):
    placed = (
        P("pair", "ints"),
        P("pair", "ints"),
        P("ints", None),
        P("ints", None, None),
        P("pair", None),
        P("pair", "ints"),
    )
    return jax.shard_map(
        local, mesh=mesh, in_specs=placed, out_specs=P("pair", "ints"), check_vma=False
    )
```

profile of v0, /device:TPU:1, one launch (start us, length us, event | category | flops | bytes accessed | tf_op | source)
XLA Modules:
  0.0 551.5 jit_solution(12331240370962497261)
XLA Ops:
  7.4 0.0 all-gather.3.cloned.1.call-start
  7.4 0.7 convert_bitcast_fusion
  8.0 0.1 broadcast_bitcast_fusion.1
  8.1 1.9 broadcast_multiply_fusion
  10.0 0.0 all-gather.3.cloned.1.call-update
  10.0 0.0 all-reduce.2.cloned.1.call-start
  10.1 0.8 reshape.30
  10.8 80.4 %all-gather.3.cloned.1.call-done = bf16[512,8192]{1,0:T(8,128)(2,1)} async-done(((bf16[512,512]{1,0:T(8,128)(2,1)}), bf16[512,8192]{1,0:T(8,128)(2,1)}) %all-gather.3.cloned.1.call-update) | async-done | bytes 8388624 | tf_op jit(solution)/shard_map/all_gather | solution.py:15
  91.2 9.3 %copy.15 = bf16[64,8,64,128]{3,2,1,0:T(8,128)(2,1)} copy(bf16[64,8,64,128]{3,1,2,0:T(8,128)(2,1)} %bitcast.55) | data formatting | bytes 16777216
  100.5 213.6 %while.12 = (s32[]{:T(128)}, f32[64,512,128]{2,0,1:T(8,128)}, s32[5,64,2]{1,0,2:T(8,128)S(1)}, bf16[512,64,128]{2,1,0:T(8,128)(2,1)}, bf16[5,64,128,128]{3,2,1,0:T(8,128)(2,1)}, /*index=5*/s32[]{:T(128)}, s32[]{:T(128)}) while((s32[]{:T(128)}, f32[64,512,128]{2,0,1:T(8,128)}, s32[5,64,2]{1,0,2:T(8,128)S(1)}, ...), condition=%wide.region_1.2_spmd.clone.clone, body=%wide.region_0.1_spmd.clone.clone.sunk | while | flops 4840235008 | bytes 94374496 | solution.py:38
  100.5 5.8 %fusion.34 = bf16[64,512,128]{2,0,1:T(8,128)(2,1)S(1)} fusion(bf16[512,64,128]{2,1,0:T(8,128)(2,1)} %get-tuple-element.146, s32[64]{0:T(128)S(1)} %get-tuple-element.127), kind=kOutput, calls=%fused_computation.12.clone.1 | convolution fusion | flops 536875008 | bytes 16777472 | tf_op jit(solution)/shard_map/while/body/eval_jaxpr/jt,ptc->jpc/dot_general | solution.py:28
  106.3 13.9 %fusion.35 = f32[64,512,128]{2,1,0:T(8,128)} fusion(bf16[64,512,128]{2,0,1:T(8,128)(2,1)S(1)} %fusion.34, bf16[5,64,128,128]{3,2,1,0:T(8,128)(2,1)} %get-tuple-element.147, s32[]{:T(128)S(6)} %copy.28), kind=kOutput, calls=%fused_computation.5.clone.1 | convolution fusion | flops 1073741824 | bytes 27262980 | tf_op jit(solution)/shard_map/while/body/eval_jaxpr/jpc,jcd->jpd/dot_general | solution.py:31
  120.2 20.4 %select_add_fusion.2 = f32[64,512,128]{2,0,1:T(8,128)} fusion(f32[64,512,128]{2,0,1:T(8,128)} %get-tuple-element.137, f32[64,512,128]{2,1,0:T(8,128)} %fusion.35, pred[]{:T(512)S(6)} %compare.3, s32[64]{0:T(128)S(1)} %get-tuple-element.128), kind=kOutput, calls=%fused_computation.4.clone.1 | convolution fusion | flops 3229618176 | bytes 50331904 | tf_op jit(solution)/shard_map/while/body/eval_jaxpr/jv,jpd->vpd/dot_general | solution.py:32
  140.6 5.8 %fusion.34 = bf16[64,512,128]{2,0,1:T(8,128)(2,1)S(1)} fusion(bf16[512,64,128]{2,1,0:T(8,128)(2,1)} %get-tuple-element.146, s32[64]{0:T(128)S(1)} %get-tuple-element.127), kind=kOutput, calls=%fused_computation.12.clone.1 | convolution fusion | flops 536875008 | bytes 16777472 | tf_op jit(solution)/shard_map/while/body/eval_jaxpr/jt,ptc->jpc/dot_general | solution.py:28
  146.4 13.9 %fusion.35 = f32[64,512,128]{2,1,0:T(8,128)} fusion(bf16[64,512,128]{2,0,1:T(8,128)(2,1)S(1)} %fusion.34, bf16[5,64,128,128]{3,2,1,0:T(8,128)(2,1)} %get-tuple-element.147, s32[]{:T(128)S(6)} %copy.28), kind=kOutput, calls=%fused_computation.5.clone.1 | convolution fusion | flops 1073741824 | bytes 27262980 | tf_op jit(solution)/shard_map/while/body/eval_jaxpr/jpc,jcd->jpd/dot_general | solution.py:31
  160.3 23.7 %select_add_fusion.2 = f32[64,512,128]{2,0,1:T(8,128)} fusion(f32[64,512,128]{2,0,1:T(8,128)} %get-tuple-element.137, f32[64,512,128]{2,1,0:T(8,128)} %fusion.35, pred[]{:T(512)S(6)} %compare.3, s32[64]{0:T(128)S(1)} %get-tuple-element.128), kind=kOutput, calls=%fused_computation.4.clone.1 | convolution fusion | flops 3229618176 | bytes 50331904 | tf_op jit(solution)/shard_map/while/body/eval_jaxpr/jv,jpd->vpd/dot_general | solution.py:32
  184.0 5.8 %fusion.34 = bf16[64,512,128]{2,0,1:T(8,128)(2,1)S(1)} fusion(bf16[512,64,128]{2,1,0:T(8,128)(2,1)} %get-tuple-element.146, s32[64]{0:T(128)S(1)} %get-tuple-element.127), kind=kOutput, calls=%fused_computation.12.clone.1 | convolution fusion | flops 536875008 | bytes 16777472 | tf_op jit(solution)/shard_map/while/body/eval_jaxpr/jt,ptc->jpc/dot_general | solution.py:28
  189.8 13.9 %fusion.35 = f32[64,512,128]{2,1,0:T(8,128)} fusion(bf16[64,512,128]{2,0,1:T(8,128)(2,1)S(1)} %fusion.34, bf16[5,64,128,128]{3,2,1,0:T(8,128)(2,1)} %get-tuple-element.147, s32[]{:T(128)S(6)} %copy.28), kind=kOutput, calls=%fused_computation.5.clone.1 | convolution fusion | flops 1073741824 | bytes 27262980 | tf_op jit(solution)/shard_map/while/body/eval_jaxpr/jpc,jcd->jpd/dot_general | solution.py:31
  203.7 23.7 %select_add_fusion.2 = f32[64,512,128]{2,0,1:T(8,128)} fusion(f32[64,512,128]{2,0,1:T(8,128)} %get-tuple-element.137, f32[64,512,128]{2,1,0:T(8,128)} %fusion.35, pred[]{:T(512)S(6)} %compare.3, s32[64]{0:T(128)S(1)} %get-tuple-element.128), kind=kOutput, calls=%fused_computation.4.clone.1 | convolution fusion | flops 3229618176 | bytes 50331904 | tf_op jit(solution)/shard_map/while/body/eval_jaxpr/jv,jpd->vpd/dot_general | solution.py:32
  227.4 5.8 %fusion.34 = bf16[64,512,128]{2,0,1:T(8,128)(2,1)S(1)} fusion(bf16[512,64,128]{2,1,0:T(8,128)(2,1)} %get-tuple-element.146, s32[64]{0:T(128)S(1)} %get-tuple-element.127), kind=kOutput, calls=%fused_computation.12.clone.1 | convolution fusion | flops 536875008 | bytes 16777472 | tf_op jit(solution)/shard_map/while/body/eval_jaxpr/jt,ptc->jpc/dot_general | solution.py:28
  233.1 13.9 %fusion.35 = f32[64,512,128]{2,1,0:T(8,128)} fusion(bf16[64,512,128]{2,0,1:T(8,128)(2,1)S(1)} %fusion.34, bf16[5,64,128,128]{3,2,1,0:T(8,128)(2,1)} %get-tuple-element.147, s32[]{:T(128)S(6)} %copy.28), kind=kOutput, calls=%fused_computation.5.clone.1 | convolution fusion | flops 1073741824 | bytes 27262980 | tf_op jit(solution)/shard_map/while/body/eval_jaxpr/jpc,jcd->jpd/dot_general | solution.py:31
  247.1 23.7 %select_add_fusion.2 = f32[64,512,128]{2,0,1:T(8,128)} fusion(f32[64,512,128]{2,0,1:T(8,128)} %get-tuple-element.137, f32[64,512,128]{2,1,0:T(8,128)} %fusion.35, pred[]{:T(512)S(6)} %compare.3, s32[64]{0:T(128)S(1)} %get-tuple-element.128), kind=kOutput, calls=%fused_computation.4.clone.1 | convolution fusion | flops 3229618176 | bytes 50331904 | tf_op jit(solution)/shard_map/while/body/eval_jaxpr/jv,jpd->vpd/dot_general | solution.py:32
  270.7 5.8 %fusion.34 = bf16[64,512,128]{2,0,1:T(8,128)(2,1)S(1)} fusion(bf16[512,64,128]{2,1,0:T(8,128)(2,1)} %get-tuple-element.146, s32[64]{0:T(128)S(1)} %get-tuple-element.127), kind=kOutput, calls=%fused_computation.12.clone.1 | convolution fusion | flops 536875008 | bytes 16777472 | tf_op jit(solution)/shard_map/while/body/eval_jaxpr/jt,ptc->jpc/dot_general | solution.py:28
  276.5 13.9 %fusion.35 = f32[64,512,128]{2,1,0:T(8,128)} fusion(bf16[64,512,128]{2,0,1:T(8,128)(2,1)S(1)} %fusion.34, bf16[5,64,128,128]{3,2,1,0:T(8,128)(2,1)} %get-tuple-element.147, s32[]{:T(128)S(6)} %copy.28), kind=kOutput, calls=%fused_computation.5.clone.1 | convolution fusion | flops 1073741824 | bytes 27262980 | tf_op jit(solution)/shard_map/while/body/eval_jaxpr/jpc,jcd->jpd/dot_general | solution.py:31
  290.4 23.7 %select_add_fusion.2 = f32[64,512,128]{2,0,1:T(8,128)} fusion(f32[64,512,128]{2,0,1:T(8,128)} %get-tuple-element.137, f32[64,512,128]{2,1,0:T(8,128)} %fusion.35, pred[]{:T(512)S(6)} %compare.3, s32[64]{0:T(128)S(1)} %get-tuple-element.128), kind=kOutput, calls=%fused_computation.4.clone.1 | convolution fusion | flops 3229618176 | bytes 50331904 | tf_op jit(solution)/shard_map/while/body/eval_jaxpr/jv,jpd->vpd/dot_general | solution.py:32
  314.1 0.0 copy-start
  314.1 0.0 all-reduce.2.cloned.1.call-update
  314.1 0.2 all-gather.5.cloned.1.call-start
  314.4 0.3 all-gather.5.cloned.1.call-update
  314.7 0.0 copy-done
  314.8 0.1 broadcast_bitcast_fusion
  314.8 219.9 %all-reduce.2.cloned.1.call-done = f32[64,512,128]{2,0,1:T(8,128)} async-done(((f32[64,512,128]{2,0,1:T(8,128)}), f32[64,512,128]{2,0,1:T(8,128)}) %all-reduce.2.cloned.1.call-update) | async-done | bytes 16777232 | tf_op jit(solution)/shard_map/psum | solution.py:39
  534.7 1.8 dynamic-slice_bitcast_fusion
  536.5 0.4 copy.10
  536.9 0.0 all-gather.5.cloned.1.call-done
  536.9 5.8 %fusion.18 = f32[512,512]{0,1:T(8,128)S(1)} fusion(f32[512,512]{0,1:T(8,128)S(1)} %bitcast.56, bf16[4096,512]{1,0:T(8,128)(2,1)} %all-gather.5.cloned.1.call-done, bf16[512,4096]{1,0:T(8,128)(2,1)} %param.12, f32[512]{0:T(512)S(1)} %broadcast_bitcast_fusion), kind=kOutput, calls=%fused_computation.21 | convolution fusion | flops 2148007936 | bytes 10487808 | tf_op jit(solution)/shard_map/dot_general | solution.py:42
  542.8 1.3 copy.11
  (12 shorter events, 0.1 us)
Async XLA Ops:
  7.4 83.8 %all-gather.3.cloned.1.call-start = ((), (), s32[]{:S(2)}) async-start(), calls=%async_computation | async-start | bytes 8912896 | tf_op jit(solution)/shard_map/all_gather | solution.py:15
  10.0 524.7 %all-reduce.2.cloned.1.call-start = ((), (), s32[]{:S(2)}) async-start(), calls=%async_computation.1 | async-start | bytes 33554432 | tf_op jit(solution)/shard_map/psum | solution.py:39
  314.1 0.7 copy-start
  314.1 222.8 %all-gather.5.cloned.1.call-start = ((), (), s32[]{:S(2)}) async-start(), calls=%async_computation.2 | async-start | bytes 4718592 | tf_op jit(solution)/shard_map/all_gather | solution.py:44
Sparse Core Ops, SparseCore 0:
  10.3 80.8 all-gather.2
  314.2 220.4 all-reduce.1
Sparse Core Ops, SparseCore 1:
  316.3 32.4 all-gather.4
where the time goes:
time: 552 us
  waiting for transfers between devices  301 us (55%)
  matrix products  219 us (40%)
  between operations  14.9 us (3%)
  local copies, waits for them, and re-layouts  13.7 us (2%)
    psum x1, waiting for transfers between devices, local(): summed = lax.psum(partial_value, 'ints')  220 us
    dot_general x5, matrix products, ladder_step(): jnp.einsum('jv,jpd->vpd', target_table, product, precision=lax.Precision....  115 us
    all_gather x1, waiting for transfers between devices, local(): block_amps = lax.all_gather(amps, 'ints', axis=1, tiled=True)  80.4 us
    dot_general x5, matrix products, ladder_step(): jnp.einsum('jpc,jcd->jpd', picked, blocks, preferred_element_type=jnp.flo...  69.7 us
    dot_general x5, matrix products, ladder_step(): jnp.einsum('jt,ptc->jpc', source_table, amps_tiled, preferred_element_typ...  28.8 us
  transfers between devices with their start and end apart: 3, of which 2 were waited for; matrix products, arithmetic and copies ran while one was open for 1% of the time, Pallas kernels for 0%

commit v1 on v0

--- a/solution.py
+++ b/solution.py
@@ -12,7 +12,24 @@
     amps = (t2.reshape(rows_here, tiles_here, tile_size) * live_mask[None, :, None]).reshape(
         rows_here, tiles_here * tile_size
     )
-    block_amps = lax.all_gather(amps, "ints", axis=1, tiled=True)
+    ways, here, step = (lax.axis_size("ints"), lax.axis_index("ints"), amps.shape[1])
+    shape = [n * ways if d == 1 else n for d, n in enumerate(amps.shape)]
+    block_amps = lax.dynamic_update_slice_in_dim(
+        jnp.zeros(shape, amps.dtype), amps, here * step, axis=1
+    )
+    going_up = going_down = amps
+    for far in range(1, ways // 2 + 1):
+        going_up = lax.ppermute(going_up, "ints", [(d, (d + 1) % ways) for d in range(ways)])
+        block_amps = lax.dynamic_update_slice_in_dim(
+            block_amps, going_up, (here - far) % ways * step, axis=1
+        )
+        if 2 * far < ways:
+            going_down = lax.ppermute(
+                going_down, "ints", [(d, (d - 1) % ways) for d in range(ways)]
+            )
+            block_amps = lax.dynamic_update_slice_in_dim(
+                block_amps, going_down, (here + far) % ways * step, axis=1
+            )
     tiles_all = block_amps.shape[1] // tile_size
     amps_tiled = block_amps.reshape(rows_here, tiles_all, tile_size)
     count_here = integrals.shape[0]

time: 552 us -> 590 us (1.069)
  starting transfers between devices: 0.27 us -> 35.3 us
  local copies, waits for them, and re-layouts: 13.7 us -> 38.9 us
  waiting for transfers between devices: 301 us -> 279 us
    all_gather x1 -> x0, waiting for transfers between devices: 80.4 us -> none  [local(): block_amps = lax.all_gather(amps, 'ints', axis=1, tiled=True)]
    ppermute x0 -> x15, waiting for transfers between devices: none -> 55.3 us  [the longest x8 55.3 us: local(): lax.ppermute(going_up, 'ints', [(d, (d + 1) % ways) for d in range(ways)])]
    ppermute x0 -> x15, starting transfers between devices: none -> 35 us  [the longest x7 32.5 us: local(): lax.ppermute(going_down, 'ints', [(d, (d - 1) % ways) for d in range(ways)])]
    dynamic_update_slice x0 -> x15, local copies, waits for them, and re-layouts: none -> 20.7 us  [the longest x8 11.2 us: local(): lax.dynamic_update_slice_in_dim(block_amps, going_up, (here - far) % ways...]
  transfers between devices with their start and end apart: 3 -> 17, of which waited for: 2 -> 8; matrix products, arithmetic and copies ran while one was open for 1% -> 4% of each run, Pallas kernels for 0% -> 0%
where the time goes in v1:
time: 590 us; the launch traced here: 589 us
  waiting for transfers between devices  279 us (47%)
  matrix products  219 us (37%)
  local copies, waits for them, and re-layouts  38.9 us (7%)
  starting transfers between devices  35.3 us (6%)
  between operations  15 us (3%)
    psum x1, waiting for transfers between devices, local(): summed = lax.psum(partial_value, 'ints')  223 us
    dot_general x5, matrix products, ladder_step(): jnp.einsum('jv,jpd->vpd', target_table, product, precision=lax.Precision....  115 us
    dot_general x5, matrix products, ladder_step(): jnp.einsum('jpc,jcd->jpd', picked, blocks, preferred_element_type=jnp.flo...  69.6 us
    ppermute x8, waiting for transfers between devices, local(): lax.ppermute(going_up, 'ints', [(d, (d + 1) % ways) for d in range(ways)])  55.3 us
    ppermute x7, starting transfers between devices, local(): lax.ppermute(going_down, 'ints', [(d, (d - 1) % ways) for d in range(ways)])  32.5 us
    dot_general x5, matrix products, ladder_step(): jnp.einsum('jt,ptc->jpc', source_table, amps_tiled, preferred_element_typ...  28.8 us
  transfers between devices with their start and end apart: 17, of which 8 were waited for; matrix products, arithmetic and copies ran while one was open for 4% of the time, Pallas kernels for 0%

profile of v1, /device:TPU:1, one launch (start us, length us, event | category | flops | bytes accessed | tf_op | source)
XLA Modules:
  0.0 588.7 jit_solution(15880532895111023995)
XLA Ops:
  8.2 4.3 broadcast_in_dim.15
  12.5 0.9 constant_dynamic-update-slice_fusion.15
  13.4 2.5 collective-permute-start
  15.9 4.5 collective-permute-start.1
  20.4 11.6 %collective-permute-done = bf16[512,512]{1,0:T(8,128)(2,1)S(1)} collective-permute-done((bf16[512,512]{1,0:T(8,128)(2,1)S(1)}, bf16[512,512]{1,0:T(8,128)(2,1)S(1)}, u32[]{:S(2)}, u32[]{:S(2)}) %collective-permute-start) | collective-permute-done | bytes 524320 | tf_op jit(solution)/shard_map/ppermute | solution.py:22
  32.1 4.8 collective-permute-start.3
  36.9 10.7 %collective-permute-done.2 = bf16[512,512]{1,0:T(8,128)(2,1)S(1)} collective-permute-done((bf16[512,512]{1,0:T(8,128)(2,1)S(1)}, bf16[512,512]{1,0:T(8,128)(2,1)S(1)}, u32[]{:S(2)}, u32[]{:S(2)}) %collective-permute-start.2) | collective-permute-done | bytes 524320 | tf_op jit(solution)/shard_map/ppermute | solution.py:22
  47.6 4.8 collective-permute-start.5
  52.4 9.7 %collective-permute-done.4 = bf16[512,512]{1,0:T(8,128)(2,1)S(1)} collective-permute-done((bf16[512,512]{1,0:T(8,128)(2,1)S(1)}, bf16[512,512]{1,0:T(8,128)(2,1)S(1)}, u32[]{:S(2)}, u32[]{:S(2)}) %collective-permute-start.4) | collective-permute-done | bytes 524320 | tf_op jit(solution)/shard_map/ppermute | solution.py:22
  62.2 4.8 collective-permute-start.7
  67.0 8.9 %collective-permute-done.6 = bf16[512,512]{1,0:T(8,128)(2,1)S(1)} collective-permute-done((bf16[512,512]{1,0:T(8,128)(2,1)S(1)}, bf16[512,512]{1,0:T(8,128)(2,1)S(1)}, u32[]{:S(2)}, u32[]{:S(2)}) %collective-permute-start.6) | collective-permute-done | bytes 524320 | tf_op jit(solution)/shard_map/ppermute | solution.py:22
  76.7 4.0 collective-permute-start.9
  80.7 8.0 %collective-permute-done.8 = bf16[512,512]{1,0:T(8,128)(2,1)} collective-permute-done((bf16[512,512]{1,0:T(8,128)(2,1)S(1)}, bf16[512,512]{1,0:T(8,128)(2,1)}, u32[]{:S(2)}, u32[]{:S(2)}) %collective-permute-start.8) | collective-permute-done | bytes 524320 | tf_op jit(solution)/shard_map/ppermute | solution.py:22
  89.6 1.9 constant_dynamic-update-slice_fusion.13
  91.6 1.9 constant_dynamic-update-slice_fusion.12
  93.5 4.7 collective-permute-start.11
  98.3 2.0 constant_dynamic-update-slice_fusion.11
  102.6 1.9 constant_dynamic-update-slice_fusion.8
  104.5 2.0 constant_dynamic-update-slice_fusion.7
  106.4 4.8 collective-permute-start.13
  111.2 1.9 constant_dynamic-update-slice_fusion.6
  113.2 0.9 constant_dynamic-update-slice_fusion.5
  114.1 1.9 constant_dynamic-update-slice_fusion.4
  116.0 0.9 constant_dynamic-update-slice_fusion.3
  116.9 0.9 constant_dynamic-update-slice_fusion.2
  117.8 0.9 constant_dynamic-update-slice_fusion.1
  118.8 5.8 collective-permute-done.14
  125.4 9.3 %copy.15 = bf16[64,8,64,128]{3,2,1,0:T(8,128)(2,1)} copy(bf16[64,8,64,128]{3,1,2,0:T(8,128)(2,1)} %bitcast.17) | data formatting | bytes 16777216
  134.8 213.5 %while.12 = (s32[]{:T(128)}, f32[64,512,128]{2,0,1:T(8,128)}, s32[5,64,2]{1,0,2:T(8,128)S(1)}, bf16[512,64,128]{2,1,0:T(8,128)(2,1)}, bf16[5,64,128,128]{3,2,1,0:T(8,128)(2,1)}, /*index=5*/s32[]{:T(128)}, s32[]{:T(128)}) while((s32[]{:T(128)}, f32[64,512,128]{2,0,1:T(8,128)}, s32[5,64,2]{1,0,2:T(8,128)S(1)}, ...), condition=%wide.region_1.2_spmd.clone.clone, body=%wide.region_0.1_spmd.clone.clone.sunk | while | flops 4840235008 | bytes 94375000 | solution.py:55
  134.8 5.8 fusion.34
  140.5 13.9 %fusion.35 = f32[64,512,128]{2,1,0:T(8,128)} fusion(bf16[64,512,128]{2,0,1:T(8,128)(2,1)S(1)} %fusion.34, bf16[5,64,128,128]{3,2,1,0:T(8,128)(2,1)} %get-tuple-element.149, s32[]{:T(128)} %get-tuple-element.138), kind=kOutput, calls=%fused_computation.5.clone.1 | convolution fusion | flops 1073741824 | bytes 27263488 | tf_op jit(solution)/shard_map/while/body/eval_jaxpr/jpc,jcd->jpd/dot_general | solution.py:48
  154.5 20.4 %select_add_fusion.2 = f32[64,512,128]{2,0,1:T(8,128)} fusion(f32[64,512,128]{2,0,1:T(8,128)} %get-tuple-element.139, f32[64,512,128]{2,1,0:T(8,128)} %fusion.35, pred[]{:T(512)S(6)} %compare.18, s32[64]{0:T(128)S(1)} %get-tuple-element.130), kind=kOutput, calls=%fused_computation.4.clone.1 | convolution fusion | flops 3229618176 | bytes 50331904 | tf_op jit(solution)/shard_map/while/body/eval_jaxpr/jv,jpd->vpd/dot_general | solution.py:49
  174.9 5.8 fusion.34
  180.7 13.9 %fusion.35 = f32[64,512,128]{2,1,0:T(8,128)} fusion(bf16[64,512,128]{2,0,1:T(8,128)(2,1)S(1)} %fusion.34, bf16[5,64,128,128]{3,2,1,0:T(8,128)(2,1)} %get-tuple-element.149, s32[]{:T(128)} %get-tuple-element.138), kind=kOutput, calls=%fused_computation.5.clone.1 | convolution fusion | flops 1073741824 | bytes 27263488 | tf_op jit(solution)/shard_map/while/body/eval_jaxpr/jpc,jcd->jpd/dot_general | solution.py:48
  194.6 23.6 %select_add_fusion.2 = f32[64,512,128]{2,0,1:T(8,128)} fusion(f32[64,512,128]{2,0,1:T(8,128)} %get-tuple-element.139, f32[64,512,128]{2,1,0:T(8,128)} %fusion.35, pred[]{:T(512)S(6)} %compare.18, s32[64]{0:T(128)S(1)} %get-tuple-element.130), kind=kOutput, calls=%fused_computation.4.clone.1 | convolution fusion | flops 3229618176 | bytes 50331904 | tf_op jit(solution)/shard_map/while/body/eval_jaxpr/jv,jpd->vpd/dot_general | solution.py:49
  218.2 5.8 fusion.34
  224.0 13.9 %fusion.35 = f32[64,512,128]{2,1,0:T(8,128)} fusion(bf16[64,512,128]{2,0,1:T(8,128)(2,1)S(1)} %fusion.34, bf16[5,64,128,128]{3,2,1,0:T(8,128)(2,1)} %get-tuple-element.149, s32[]{:T(128)} %get-tuple-element.138), kind=kOutput, calls=%fused_computation.5.clone.1 | convolution fusion | flops 1073741824 | bytes 27263488 | tf_op jit(solution)/shard_map/while/body/eval_jaxpr/jpc,jcd->jpd/dot_general | solution.py:48
  237.9 23.6 %select_add_fusion.2 = f32[64,512,128]{2,0,1:T(8,128)} fusion(f32[64,512,128]{2,0,1:T(8,128)} %get-tuple-element.139, f32[64,512,128]{2,1,0:T(8,128)} %fusion.35, pred[]{:T(512)S(6)} %compare.18, s32[64]{0:T(128)S(1)} %get-tuple-element.130), kind=kOutput, calls=%fused_computation.4.clone.1 | convolution fusion | flops 3229618176 | bytes 50331904 | tf_op jit(solution)/shard_map/while/body/eval_jaxpr/jv,jpd->vpd/dot_general | solution.py:49
  261.6 5.8 fusion.34
  267.4 13.9 %fusion.35 = f32[64,512,128]{2,1,0:T(8,128)} fusion(bf16[64,512,128]{2,0,1:T(8,128)(2,1)S(1)} %fusion.34, bf16[5,64,128,128]{3,2,1,0:T(8,128)(2,1)} %get-tuple-element.149, s32[]{:T(128)} %get-tuple-element.138), kind=kOutput, calls=%fused_computation.5.clone.1 | convolution fusion | flops 1073741824 | bytes 27263488 | tf_op jit(solution)/shard_map/while/body/eval_jaxpr/jpc,jcd->jpd/dot_general | solution.py:48
  281.3 23.6 %select_add_fusion.2 = f32[64,512,128]{2,0,1:T(8,128)} fusion(f32[64,512,128]{2,0,1:T(8,128)} %get-tuple-element.139, f32[64,512,128]{2,1,0:T(8,128)} %fusion.35, pred[]{:T(512)S(6)} %compare.18, s32[64]{0:T(128)S(1)} %get-tuple-element.130), kind=kOutput, calls=%fused_computation.4.clone.1 | convolution fusion | flops 3229618176 | bytes 50331904 | tf_op jit(solution)/shard_map/while/body/eval_jaxpr/jv,jpd->vpd/dot_general | solution.py:49
  304.9 5.8 fusion.34
  310.7 13.9 %fusion.35 = f32[64,512,128]{2,1,0:T(8,128)} fusion(bf16[64,512,128]{2,0,1:T(8,128)(2,1)S(1)} %fusion.34, bf16[5,64,128,128]{3,2,1,0:T(8,128)(2,1)} %get-tuple-element.149, s32[]{:T(128)} %get-tuple-element.138), kind=kOutput, calls=%fused_computation.5.clone.1 | convolution fusion | flops 1073741824 | bytes 27263488 | tf_op jit(solution)/shard_map/while/body/eval_jaxpr/jpc,jcd->jpd/dot_general | solution.py:48
  324.6 23.6 %select_add_fusion.2 = f32[64,512,128]{2,0,1:T(8,128)} fusion(f32[64,512,128]{2,0,1:T(8,128)} %get-tuple-element.139, f32[64,512,128]{2,1,0:T(8,128)} %fusion.35, pred[]{:T(512)S(6)} %compare.18, s32[64]{0:T(128)S(1)} %get-tuple-element.130), kind=kOutput, calls=%fused_computation.4.clone.1 | convolution fusion | flops 3229618176 | bytes 50331904 | tf_op jit(solution)/shard_map/while/body/eval_jaxpr/jv,jpd->vpd/dot_general | solution.py:49
  349.0 223.0 %all-reduce.2.cloned.1.call-done = f32[64,512,128]{2,0,1:T(8,128)} async-done(((f32[64,512,128]{2,0,1:T(8,128)}), f32[64,512,128]{2,0,1:T(8,128)}) %all-reduce.2.cloned.1.call-update) | async-done | bytes 16777232 | tf_op jit(solution)/shard_map/psum | solution.py:56
  571.9 1.8 dynamic-slice_bitcast_fusion
  574.1 5.8 fusion.18
  580.0 1.3 copy.11
  (58 shorter events, 7.0 us)
Async XLA Ops:
  7.4 5.1 copy-start.1
  7.4 81.3 %copy-start.6 = (s32[320,2]{0,1:T(2,128)S(1)}, s32[320,2]{0,1:T(2,128)}, u32[]{:S(2)}) copy-start(s32[320,2]{0,1:T(2,128)} %param.10) | copy-start | bytes 7684
  7.4 564.6 %all-reduce.2.cloned.1.call-start = ((), (), s32[]{:S(2)}) async-start(), calls=%async_computation | async-start | bytes 33554432 | tf_op jit(solution)/shard_map/psum | solution.py:56
  13.4 121.4 %copy-start = (bf16[512,512]{1,0:T(8,128)(2,1)}, bf16[512,512]{1,0:T(8,128)(2,1)S(1)}, u32[]{:S(2)}) copy-start(bf16[512,512]{1,0:T(8,128)(2,1)S(1)} %get-tuple-element.93) | copy-start | bytes 1572868
  13.4 18.7 %collective-permute-start = (bf16[512,512]{1,0:T(8,128)(2,1)S(1)}, bf16[512,512]{1,0:T(8,128)(2,1)S(1)}, u32[]{:S(2)}, u32[]{:S(2)}) collective-permute-start(bf16[512,512]{1,0:T(8,128)(2,1)S(1)} %get-tuple-element.93), channel_id=1, source_target_pairs={{0,1},{1,2},{2,3},{3,4},{4,5},{5,6},{6,7},{7,8},{8,9},{9,10},{10,1... | collective-permute-start | bytes 1572872 | tf_op jit(solution)/shard_map/ppermute | solution.py:22
  15.9 16.2 %collective-permute-start.1 = (bf16[512,512]{1,0:T(8,128)(2,1)S(1)}, bf16[512,512]{1,0:T(8,128)(2,1)S(1)}, u32[]{:S(2)}, u32[]{:S(2)}) collective-permute-start(bf16[512,512]{1,0:T(8,128)(2,1)S(1)} %get-tuple-element.93), channel_id=1, source_target_pairs={{0,15},{1,0},{2,1},{3,2},{4,3},{5,4},{6,5},{7,6},{8,7},{9,8},{10,9... | collective-permute-start | bytes 1572872 | tf_op jit(solution)/shard_map/ppermute | solution.py:27
  32.1 15.5 %collective-permute-start.2 = (bf16[512,512]{1,0:T(8,128)(2,1)S(1)}, bf16[512,512]{1,0:T(8,128)(2,1)S(1)}, u32[]{:S(2)}, u32[]{:S(2)}) collective-permute-start(bf16[512,512]{1,0:T(8,128)(2,1)S(1)} %collective-permute-done), channel_id=1, source_target_pairs={{0,1},{1,2},{2,3},{3,4},{4,5},{5,6},{6,7},{7,8},{8,9},{9,10},{10,1... | collective-permute-start | bytes 1572872 | tf_op jit(solution)/shard_map/ppermute | solution.py:22
  32.1 15.5 %copy-start.3 = (bf16[512,512]{1,0:T(8,128)(2,1)}, bf16[512,512]{1,0:T(8,128)(2,1)S(1)}, u32[]{:S(2)}) copy-start(bf16[512,512]{1,0:T(8,128)(2,1)S(1)} %collective-permute-done.1) | copy-start | bytes 1572868
  32.1 15.5 %collective-permute-start.3 = (bf16[512,512]{1,0:T(8,128)(2,1)S(1)}, bf16[512,512]{1,0:T(8,128)(2,1)S(1)}, u32[]{:S(2)}, u32[]{:S(2)}) collective-permute-start(bf16[512,512]{1,0:T(8,128)(2,1)S(1)} %collective-permute-done.1), channel_id=1, source_target_pairs={{0,15},{1,0},{2,1},{3,2},{4,3},{5,4},{6,5},{7,6},{8,7},{9,8},{10,9... | collective-permute-start | bytes 1572872 | tf_op jit(solution)/shard_map/ppermute | solution.py:27
  47.6 4.9 copy-start.5
  47.6 14.6 %collective-permute-start.4 = (bf16[512,512]{1,0:T(8,128)(2,1)S(1)}, bf16[512,512]{1,0:T(8,128)(2,1)S(1)}, u32[]{:S(2)}, u32[]{:S(2)}) collective-permute-start(bf16[512,512]{1,0:T(8,128)(2,1)S(1)} %collective-permute-done.2), channel_id=1, source_target_pairs={{0,1},{1,2},{2,3},{3,4},{4,5},{5,6},{6,7},{7,8},{8,9},{9,10},{10,1... | collective-permute-start | bytes 1572872 | tf_op jit(solution)/shard_map/ppermute | solution.py:22
  47.6 28.2 %copy-start.2 = (bf16[512,512]{1,0:T(8,128)(2,1)}, bf16[512,512]{1,0:T(8,128)(2,1)S(1)}, u32[]{:S(2)}) copy-start(bf16[512,512]{1,0:T(8,128)(2,1)S(1)} %collective-permute-done.3) | copy-start | bytes 1572868
  47.6 14.6 %collective-permute-start.5 = (bf16[512,512]{1,0:T(8,128)(2,1)S(1)}, bf16[512,512]{1,0:T(8,128)(2,1)S(1)}, u32[]{:S(2)}, u32[]{:S(2)}) collective-permute-start(bf16[512,512]{1,0:T(8,128)(2,1)S(1)} %collective-permute-done.3), channel_id=1, source_target_pairs={{0,15},{1,0},{2,1},{3,2},{4,3},{5,4},{6,5},{7,6},{8,7},{9,8},{10,9... | collective-permute-start | bytes 1572872 | tf_op jit(solution)/shard_map/ppermute | solution.py:27
  62.2 13.7 %collective-permute-start.6 = (bf16[512,512]{1,0:T(8,128)(2,1)S(1)}, bf16[512,512]{1,0:T(8,128)(2,1)S(1)}, u32[]{:S(2)}, u32[]{:S(2)}) collective-permute-start(bf16[512,512]{1,0:T(8,128)(2,1)S(1)} %collective-permute-done.4), channel_id=1, source_target_pairs={{0,1},{1,2},{2,3},{3,4},{4,5},{5,6},{6,7},{7,8},{8,9},{9,10},{10,1... | collective-permute-start | bytes 1572872 | tf_op jit(solution)/shard_map/ppermute | solution.py:22
  62.2 13.7 %collective-permute-start.7 = (bf16[512,512]{1,0:T(8,128)(2,1)S(1)}, bf16[512,512]{1,0:T(8,128)(2,1)}, u32[]{:S(2)}, u32[]{:S(2)}) collective-permute-start(bf16[512,512]{1,0:T(8,128)(2,1)S(1)} %collective-permute-done.5), channel_id=1, source_target_pairs={{0,15},{1,0},{2,1},{3,2},{4,3},{5,4},{6,5},{7,6},{8,7},{9,8},{10,9... | collective-permute-start | bytes 1572872 | tf_op jit(solution)/shard_map/ppermute | solution.py:27
  75.8 0.8 copy-start.4
  75.8 12.8 %collective-permute-start.8 = (bf16[512,512]{1,0:T(8,128)(2,1)S(1)}, bf16[512,512]{1,0:T(8,128)(2,1)}, u32[]{:S(2)}, u32[]{:S(2)}) collective-permute-start(bf16[512,512]{1,0:T(8,128)(2,1)S(1)} %collective-permute-done.6), channel_id=1, source_target_pairs={{0,1},{1,2},{2,3},{3,4},{4,5},{5,6},{6,7},{7,8},{8,9},{9,10},{10,1... | collective-permute-start | bytes 1572872 | tf_op jit(solution)/shard_map/ppermute | solution.py:22
  76.7 16.8 %collective-permute-start.9 = (bf16[512,512]{1,0:T(8,128)(2,1)}, bf16[512,512]{1,0:T(8,128)(2,1)S(1)}, u32[]{:S(2)}, u32[]{:S(2)}) collective-permute-start(bf16[512,512]{1,0:T(8,128)(2,1)} %collective-permute-done.7), channel_id=1, source_target_pairs={{0,15},{1,0},{2,1},{3,2},{4,3},{5,4},{6,5},{7,6},{8,7},{9,8},{10,9... | collective-permute-start | bytes 1572872 | tf_op jit(solution)/shard_map/ppermute | solution.py:27
  88.7 12.1 %collective-permute-start.10 = (bf16[512,512]{1,0:T(8,128)(2,1)}, bf16[512,512]{1,0:T(8,128)(2,1)}, u32[]{:S(2)}, u32[]{:S(2)}) collective-permute-start(bf16[512,512]{1,0:T(8,128)(2,1)} %collective-permute-done.8), channel_id=1, source_target_pairs={{0,1},{1,2},{2,3},{3,4},{4,5},{5,6},{6,7},{7,8},{8,9},{9,10},{10,1... | collective-permute-start | bytes 1572872 | tf_op jit(solution)/shard_map/ppermute | solution.py:22
  93.5 12.9 %collective-permute-start.11 = (bf16[512,512]{1,0:T(8,128)(2,1)S(1)}, bf16[512,512]{1,0:T(8,128)(2,1)S(1)}, u32[]{:S(2)}, u32[]{:S(2)}) collective-permute-start(bf16[512,512]{1,0:T(8,128)(2,1)S(1)} %collective-permute-done.9), channel_id=1, source_target_pairs={{0,15},{1,0},{2,1},{3,2},{4,3},{5,4},{6,5},{7,6},{8,7},{9,8},{10,9... | collective-permute-start | bytes 1572872 | tf_op jit(solution)/shard_map/ppermute | solution.py:27
  100.8 12.4 %collective-permute-start.12 = (bf16[512,512]{1,0:T(8,128)(2,1)}, bf16[512,512]{1,0:T(8,128)(2,1)S(1)}, u32[]{:S(2)}, u32[]{:S(2)}) collective-permute-start(bf16[512,512]{1,0:T(8,128)(2,1)} %collective-permute-done.10), channel_id=1, source_target_pairs={{0,1},{1,2},{2,3},{3,4},{4,5},{5,6},{6,7},{7,8},{8,9},{9,10},{10,1... | collective-permute-start | bytes 1572872 | tf_op jit(solution)/shard_map/ppermute | solution.py:22
  106.4 11.4 %collective-permute-start.13 = (bf16[512,512]{1,0:T(8,128)(2,1)S(1)}, bf16[512,512]{1,0:T(8,128)(2,1)S(1)}, u32[]{:S(2)}, u32[]{:S(2)}) collective-permute-start(bf16[512,512]{1,0:T(8,128)(2,1)S(1)} %collective-permute-done.11), channel_id=1, source_target_pairs={{0,15},{1,0},{2,1},{3,2},{4,3},{5,4},{6,5},{7,6},{8,7},{9,8},{10,9... | collective-permute-start | bytes 1572872 | tf_op jit(solution)/shard_map/ppermute | solution.py:27
  113.2 11.4 %collective-permute-start.14 = (bf16[512,512]{1,0:T(8,128)(2,1)S(1)}, bf16[512,512]{1,0:T(8,128)(2,1)S(1)}, u32[]{:S(2)}, u32[]{:S(2)}) collective-permute-start(bf16[512,512]{1,0:T(8,128)(2,1)S(1)} %collective-permute-done.12), channel_id=1, source_target_pairs={{0,1},{1,2},{2,3},{3,4},{4,5},{5,6},{6,7},{7,8},{8,9},{9,10},{10,1... | collective-permute-start | bytes 1572872 | tf_op jit(solution)/shard_map/ppermute | solution.py:22
  348.3 0.7 copy-start.7
  348.3 225.8 %all-gather.2.cloned.1.call-start = ((), (), s32[]{:S(2)}) async-start(), calls=%async_computation.1 | async-start | bytes 4718592 | tf_op jit(solution)/shard_map/all_gather | solution.py:61
Sparse Core Ops, SparseCore 0:
  348.4 223.4 all-reduce.1
Sparse Core Ops, SparseCore 1:
  350.5 35.4 all-gather.1
